TPU v7x, 256 devices: a whole 4x4x8 slice. The times are simulated.
256 devices in a mesh: dp: 2 (over core), ctx: 128 (over x, z, y).
Axes of the slice: x: 4, y: 4, z: 8, core: 2. Of those that a mesh axis runs over, the one named last changes fastest.
Arguments:
- queries: bfloat16 [2, 16384, 2048], P('dp', 'ctx'), may hold values from -6 to 6
- keys: bfloat16 [2, 16384, 2048], P('dp', 'ctx'), may hold values from -6 to 6
- values: bfloat16 [2, 16384, 2048], P('dp', 'ctx'), may hold values from -6 to 6
- doc_ids: int32 [2, 256], P('dp', 'ctx'), may hold values from 0 to 7, never falling along the last dimension, each value on 1 to 64 neighbouring positions
- feat_weight: bfloat16 [128, 160], replicated, may hold values from -0.5 to 0.5
- out_grad: bfloat16 [2, 16384, 2048], P('dp', 'ctx'), may hold values from -6 to 6
Outputs:
- out: float32 [2, 16384, 2048], P('dp', 'ctx')
- query_grad: float32 [2, 16384, 2048], P('dp', 'ctx')
- key_grad: float32 [2, 16384, 2048], P('dp', 'ctx')
- value_grad: float32 [2, 16384, 2048], P('dp', 'ctx')
- new_weight: float32 [128, 160], replicated
Inputs may be any that keep to these rules, and one draw needn't show every extreme that they name: `doc_ids`: along each sequence the ids never fall; every id names one run of 1 to 64 blocks, and one run has exactly 64 blocks.
All inputs are finite; a program needn't handle non-finite values.
Results may differ from a plain program's by a relative error of at most 0.015.
Values sent between devices are 32-bit elements; how exact they have to be, the bound alone decides.
No kernel may reach another device: no remote copies, remote signals or barrier semaphores. Data moves between devices by JAX's collectives and lax.ppermute only.
A program may use at most 64 MiB of HBM per device.

v0:
```python
import math
import jax
import jax.numpy as jnp
from jax import lax
from jax.sharding import PartitionSpec as P

H = 16
DH = 128
F = 160
BLOCK = 64
HIGH = lax.Precision.HIGHEST
RATE = 0.5
EPSILON = 1e-06


def passed_along(array, axis, by):
    length = lax.axis_size(axis)
    pairs = [(i, i + by) for i in range(length) if 0 <= i + by < length]
    return lax.ppermute(array, axis, pairs)


def features(proj):
    return (1.0 + proj + 0.5 * proj * proj).astype(jnp.bfloat16)


def pack_parts(parts):
    return jnp.concatenate([part.reshape(-1) for part in parts])


def unpack_parts(packed, shapes):
    result = []
    offset = 0
    for shape in shapes:
        length = math.prod(shape)
        result.append(packed[offset : offset + length].reshape(shape))
        offset = offset + length
    return result


def chain_combine(earlier, later):
    joined = later[0] == earlier[0]
    merged = later[1:] + jnp.where(joined, earlier[1:], jnp.zeros_like(earlier[1:]))
    return jnp.concatenate([later[:1], merged])


def prefix(packed, reverse, mover):
    count = lax.axis_size("ctx")
    index = lax.axis_index("ctx")
    blank = jnp.zeros_like(packed).at[0].set(-1.0)
    sign = -1 if reverse else 1

    def valid(step):
        if reverse:
            return index < count - step
        return index >= step

    total = jnp.where(valid(1), mover(packed, sign), blank)
    step = 1
    while step < count:
        got = mover(total, sign * step)
        total = jnp.where(valid(step), chain_combine(got, total), total)
        step = step * 2
    return total


def state_mover(value, by):
    return passed_along(value, "ctx", by)


def adjoint_mover(value, by):
    return passed_along(value, "ctx", by)


def shards(queries, keys, values, doc_ids, feat_weight, out_grad):
    tokens = queries.shape[1]
    query3 = queries.reshape(tokens, H, DH)
    key3 = keys.reshape(tokens, H, DH)
    value3 = values.reshape(tokens, H, DH)
    grad3 = out_grad.reshape(tokens, H, DH).astype(jnp.float32)
    blocks = doc_ids.shape[1]
    docs = jnp.broadcast_to(doc_ids[0][:, None], (blocks, BLOCK)).reshape(tokens)
    doc_float = docs.astype(jnp.float32)
    proj_q = jnp.einsum("thd,df->thf", query3, feat_weight, preferred_element_type=jnp.float32)
    proj_k = jnp.einsum("thd,df->thf", key3, feat_weight, preferred_element_type=jnp.float32)
    feat_q = features(proj_q)
    feat_k = features(proj_k)
    order = jnp.arange(tokens)
    mask = jnp.logical_and(order[None, :] <= order[:, None], docs[None, :] == docs[:, None]).astype(
        jnp.float32
    )
    raw = jnp.einsum("thf,shf->hts", feat_q, feat_k, preferred_element_type=jnp.float32)
    probs = (raw * mask[None]).astype(jnp.bfloat16)
    num_local = jnp.einsum("hts,shd->thd", probs, value3, preferred_element_type=jnp.float32)
    den_local = jnp.sum(probs, axis=2, dtype=jnp.float32).T
    feat_qf = feat_q.astype(jnp.float32)
    feat_kf = feat_k.astype(jnp.float32)
    value_f = value3.astype(jnp.float32)
    tail_mask = (docs == docs[-1]).astype(jnp.float32)
    head_mask = (docs == docs[0]).astype(jnp.float32)
    tail_state = jnp.einsum(
        "thf,thd->hfd",
        feat_k * tail_mask.astype(jnp.bfloat16)[:, None, None],
        value3,
        preferred_element_type=jnp.float32,
    )
    tail_norm = jnp.einsum("thf,t->hf", feat_kf, tail_mask, precision=HIGH)
    last_doc = doc_float[-1:]
    first_doc = doc_float[:1]
    head_feat = feat_qf * head_mask[:, None, None]
    state_shape = (H, F, DH)
    norm_shape = (H, F)
    forward_sums = prefix(pack_parts([last_doc, tail_state, tail_norm]), False, state_mover)
    pre_doc, state_in, norm_in = unpack_parts(forward_sums, [(1,), state_shape, norm_shape])
    pre_end = pre_doc[0]
    in_mask = (doc_float == pre_end).astype(jnp.float32)
    den = den_local + jnp.einsum("thf,hf->th", feat_qf, norm_in, precision=HIGH) * in_mask[:, None]
    scaled = grad3 / den[:, :, None]
    head_state = jnp.einsum("thf,thd->hfd", head_feat, scaled, precision=HIGH)
    in_mask, den, scaled, head_state = (in_mask, den, scaled, head_state)
    out = (
        num_local
        + jnp.einsum("thf,hfd->thd", feat_qf, state_in, precision=HIGH) * in_mask[:, None, None]
    ) / den[:, :, None]
    drift = -jnp.sum(grad3 * out, axis=2) / den
    head_norm = jnp.einsum("thf,th->hf", head_feat, drift, precision=HIGH)
    out, drift, head_norm = (out, drift, head_norm)
    backward_sums = prefix(pack_parts([first_doc, head_state, head_norm]), True, adjoint_mover)
    post_doc, adjoint, adjoint_norm = unpack_parts(backward_sums, [(1,), state_shape, norm_shape])
    suffix_doc = post_doc[0]
    scaled_b = scaled.astype(jnp.bfloat16)
    dscore = (
        jnp.einsum("thd,shd->hts", scaled_b, value3, preferred_element_type=jnp.float32)
        + drift.T[:, :, None]
    )
    dprobs = (dscore * mask[None]).astype(jnp.bfloat16)
    out_mask = (doc_float == suffix_doc).astype(jnp.float32)
    grad_fq = (
        jnp.einsum("hts,shf->thf", dprobs, feat_k, preferred_element_type=jnp.float32)
        + (
            jnp.einsum("hfd,thd->thf", state_in, scaled, precision=HIGH)
            + norm_in[None] * drift[:, :, None]
        )
        * in_mask[:, None, None]
    )
    grad_fk = (
        jnp.einsum("hts,thf->shf", dprobs, feat_q, preferred_element_type=jnp.float32)
        + (jnp.einsum("hfd,shd->shf", adjoint, value_f, precision=HIGH) + adjoint_norm[None])
        * out_mask[:, None, None]
    )
    value_grad = (
        jnp.einsum("hts,thd->shd", probs, scaled_b, preferred_element_type=jnp.float32)
        + jnp.einsum("shf,hfd->shd", feat_kf, adjoint, precision=HIGH) * out_mask[:, None, None]
    )
    grad_pq = (grad_fq * (1.0 + proj_q)).astype(jnp.bfloat16)
    grad_pk = (grad_fk * (1.0 + proj_k)).astype(jnp.bfloat16)
    query_grad = jnp.einsum("thf,df->thd", grad_pq, feat_weight, preferred_element_type=jnp.float32)
    key_grad = jnp.einsum("thf,df->thd", grad_pk, feat_weight, preferred_element_type=jnp.float32)
    weight_part = jnp.einsum(
        "thd,thf->df", query3, grad_pq, preferred_element_type=jnp.float32
    ) + jnp.einsum("thd,thf->df", key3, grad_pk, preferred_element_type=jnp.float32)
    weight_grad = lax.psum(weight_part, ("dp", "ctx"))
    scale = lax.rsqrt(jnp.mean(weight_grad * weight_grad) + EPSILON)
    new_weight = feat_weight.astype(jnp.float32) - RATE * weight_grad * scale
    shape_out = (1, tokens, H * DH)
    return (
        out.reshape(shape_out),
        query_grad.reshape(shape_out),
        key_grad.reshape(shape_out),
        value_grad.reshape(shape_out),
        new_weight,
    )


def solution(mesh):
    placed = (
        P("dp", "ctx", None),
        P("dp", "ctx", None),
        P("dp", "ctx", None),
        P("dp", "ctx"),
        P(),
        P("dp", "ctx", None),
    )
    return jax.shard_map(
        shards,
        mesh=mesh,
        in_specs=placed,
        out_specs=(
            P("dp", "ctx", None),
            P("dp", "ctx", None),
            P("dp", "ctx", None),
            P("dp", "ctx", None),
            P(),
        ),
        check_vma=False,
    )
```

profile of v0, /device:TPU:1, one launch (start us, length us, event | category | flops | bytes accessed | tf_op | source)
XLA Modules:
  0.0 1037.0 jit_solution(11877758748306444700)
XLA Ops:
  14.5 10.6 %concatenate.51 = f32[330241]{0:T(1024)} concatenate(f32[1]{0:T(128)} %get-tuple-element.35, f32[327680]{0:T(1024)S(1)} %bitcast.136, f32[2560]{0:T(1024)S(1)} %convolution_reduce_fusion), dimensions={0} | concatenate | bytes 2641928 | tf_op jit(solution)/shard_map/concatenate | solution.py:27
  29.2 27.9 %collective-permute-done = f32[330241]{0:T(1024)S(1)} collective-permute-done((f32[330241]{0:T(1024)}, f32[330241]{0:T(1024)S(1)}, u32[]{:S(2)}, u32[]{:S(2)}) %collective-permute-start) | collective-permute-done | bytes 1320996 | tf_op jit(solution)/shard_map/ppermute | solution.py:19
  62.8 26.3 %collective-permute-done.1 = f32[330241]{0:T(1024)S(1)} collective-permute-done((f32[330241]{0:T(1024)S(1)}, f32[330241]{0:T(1024)S(1)}, u32[]{:S(2)}, u32[]{:S(2)}) %collective-permute-start.1) | collective-permute-done | bytes 1320996 | tf_op jit(solution)/shard_map/ppermute | solution.py:19
  93.3 6.8 collective-permute-start.2
  100.6 24.4 %collective-permute-done.2 = f32[330241]{0:T(1024)} collective-permute-done((f32[330241]{0:T(1024)S(1)}, f32[330241]{0:T(1024)}, u32[]{:S(2)}, u32[]{:S(2)}) %collective-permute-start.2) | collective-permute-done | bytes 1320996 | tf_op jit(solution)/shard_map/ppermute | solution.py:19
  132.1 9.4 collective-permute-start.3
  141.9 23.5 %collective-permute-done.3 = f32[330241]{0:T(1024)} collective-permute-done((f32[330241]{0:T(1024)S(1)}, f32[330241]{0:T(1024)}, u32[]{:S(2)}, u32[]{:S(2)}) %collective-permute-start.3) | collective-permute-done | bytes 1320996 | tf_op jit(solution)/shard_map/ppermute | solution.py:19
  179.1 42.0 %collective-permute-done.4 = f32[330241]{0:T(1024)S(1)} collective-permute-done((f32[330241]{0:T(1024)}, f32[330241]{0:T(1024)S(1)}, u32[]{:S(2)}, u32[]{:S(2)}) %collective-permute-start.4) | collective-permute-done | bytes 1320996 | tf_op jit(solution)/shard_map/ppermute | solution.py:19
  227.4 25.8 %collective-permute-start.5 = (f32[330241]{0:T(1024)S(1)}, f32[330241]{0:T(1024)}, u32[]{:S(2)}, u32[]{:S(2)}) collective-permute-start(f32[330241]{0:T(1024)S(1)} %maximum_select_fusion.3), channel_id=1, source_target_pairs={{0,16},{1,17},{2,18},{3,19},{4,20},{5,21},{6,22},{7,23},{8,24},{9,... | collective-permute-start | bytes 3962900 | tf_op jit(solution)/shard_map/ppermute | solution.py:19
  253.7 33.4 %collective-permute-done.5 = f32[330241]{0:T(1024)} collective-permute-done((f32[330241]{0:T(1024)S(1)}, f32[330241]{0:T(1024)}, u32[]{:S(2)}, u32[]{:S(2)}) %collective-permute-start.5) | collective-permute-done | bytes 1320996 | tf_op jit(solution)/shard_map/ppermute | solution.py:19
  293.9 13.6 %collective-permute-start.6 = (f32[330241]{0:T(1024)}, f32[330241]{0:T(1024)S(1)}, u32[]{:S(2)}, u32[]{:S(2)}) collective-permute-start(f32[330241]{0:T(1024)} %maximum_select_fusion.4), channel_id=1, source_target_pairs={{0,32},{1,33},{2,34},{3,35},{4,36},{5,37},{6,38},{7,39},{8,40},{9,... | collective-permute-start | bytes 3962900 | tf_op jit(solution)/shard_map/ppermute | solution.py:19
  308.7 15.0 %collective-permute-done.6 = f32[330241]{0:T(1024)S(1)} collective-permute-done((f32[330241]{0:T(1024)}, f32[330241]{0:T(1024)S(1)}, u32[]{:S(2)}, u32[]{:S(2)}) %collective-permute-start.6) | collective-permute-done | bytes 1320996 | tf_op jit(solution)/shard_map/ppermute | solution.py:19
  330.0 33.4 %collective-permute-start.7 = (f32[330241]{0:T(1024)S(1)}, f32[330241]{0:T(1024)}, u32[]{:S(2)}, u32[]{:S(2)}) collective-permute-start(f32[330241]{0:T(1024)S(1)} %maximum_select_fusion.5), channel_id=1, source_target_pairs={{0,64},{1,65},{2,66},{3,67},{4,68},{5,69},{6,70},{7,71},{8,72},{9,... | collective-permute-start | bytes 3962900 | tf_op jit(solution)/shard_map/ppermute | solution.py:19
  372.0 16.8 %collective-permute-done.7 = f32[330241]{0:T(1024)} collective-permute-done((f32[330241]{0:T(1024)S(1)}, f32[330241]{0:T(1024)}, u32[]{:S(2)}, u32[]{:S(2)}) %collective-permute-start.7) | collective-permute-done | bytes 1320996 | tf_op jit(solution)/shard_map/ppermute | solution.py:19
  409.1 13.9 %concatenate.59 = f32[330241]{0:T(1024)} concatenate(f32[1]{0:T(128)} %get-tuple-element.34, f32[327680]{0:T(1024)} %bitcast.149, f32[2560]{0:T(1024)S(1)} %reshape.197), dimensions={0} | concatenate | bytes 2641928 | tf_op jit(solution)/shard_map/concatenate | solution.py:27
  424.3 29.2 %collective-permute-done.8 = f32[330241]{0:T(1024)S(1)} collective-permute-done((f32[330241]{0:T(1024)}, f32[330241]{0:T(1024)S(1)}, u32[]{:S(2)}, u32[]{:S(2)}) %collective-permute-start.8) | collective-permute-done | bytes 1320996 | tf_op jit(solution)/shard_map/ppermute | solution.py:19
  456.4 27.6 %collective-permute-done.9 = f32[330241]{0:T(1024)S(1)} collective-permute-done((f32[330241]{0:T(1024)S(1)}, f32[330241]{0:T(1024)S(1)}, u32[]{:S(2)}, u32[]{:S(2)}) %collective-permute-start.9) | collective-permute-done | bytes 1320996 | tf_op jit(solution)/shard_map/ppermute | solution.py:19
  490.0 28.2 %collective-permute-done.10 = f32[330241]{0:T(1024)S(1)} collective-permute-done((f32[330241]{0:T(1024)S(1)}, f32[330241]{0:T(1024)S(1)}, u32[]{:S(2)}, u32[]{:S(2)}) %collective-permute-start.10) | collective-permute-done | bytes 1320996 | tf_op jit(solution)/shard_map/ppermute | solution.py:19
  524.0 25.7 %collective-permute-done.11 = f32[330241]{0:T(1024)S(1)} collective-permute-done((f32[330241]{0:T(1024)S(1)}, f32[330241]{0:T(1024)S(1)}, u32[]{:S(2)}, u32[]{:S(2)}) %collective-permute-start.11) | collective-permute-done | bytes 1320996 | tf_op jit(solution)/shard_map/ppermute | solution.py:19
  555.1 56.0 %collective-permute-done.12 = f32[330241]{0:T(1024)S(1)} collective-permute-done((f32[330241]{0:T(1024)S(1)}, f32[330241]{0:T(1024)S(1)}, u32[]{:S(2)}, u32[]{:S(2)}) %collective-permute-start.12) | collective-permute-done | bytes 1320996 | tf_op jit(solution)/shard_map/ppermute | solution.py:19
  616.6 30.2 %collective-permute-done.13 = f32[330241]{0:T(1024)S(1)} collective-permute-done((f32[330241]{0:T(1024)S(1)}, f32[330241]{0:T(1024)S(1)}, u32[]{:S(2)}, u32[]{:S(2)}) %collective-permute-start.13) | collective-permute-done | bytes 1320996 | tf_op jit(solution)/shard_map/ppermute | solution.py:19
  656.6 41.9 %collective-permute-done.14 = f32[330241]{0:T(1024)S(1)} collective-permute-done((f32[330241]{0:T(1024)S(1)}, f32[330241]{0:T(1024)S(1)}, u32[]{:S(2)}, u32[]{:S(2)}) %collective-permute-start.14) | collective-permute-done | bytes 1320996 | tf_op jit(solution)/shard_map/ppermute | solution.py:19
  716.4 36.3 %collective-permute-done.15 = f32[330241]{0:T(1024)} collective-permute-done((f32[330241]{0:T(1024)S(1)}, f32[330241]{0:T(1024)}, u32[]{:S(2)}, u32[]{:S(2)}) %collective-permute-start.15) | collective-permute-done | bytes 1320996 | tf_op jit(solution)/shard_map/ppermute | solution.py:19
  771.6 254.6 %all-reduce.2.cloned.1.call-done = f32[128,160]{0,1:T(8,128)} async-done(((f32[128,160]{0,1:T(8,128)}), f32[128,160]{0,1:T(8,128)}) %all-reduce.2.cloned.1.call-update) | async-done | bytes 81936 | tf_op jit(solution)/shard_map/psum | solution.py:161
  (199 shorter events, 150.5 us)
Async XLA Ops:
  7.2 5.4 copy-start.27
  7.2 5.5 copy-start.25
  7.2 1019.0 %all-reduce.2.cloned.1.call-start = ((), (), s32[]{:S(2)}) async-start(), calls=%async_computation | async-start | bytes 163840 | tf_op jit(solution)/shard_map/psum | solution.py:161
  14.5 42.7 %copy-start = (f32[330241]{0:T(1024)S(1)}, f32[330241]{0:T(1024)}, u32[]{:S(2)}) copy-start(f32[330241]{0:T(1024)} %constant.75.clone.1) | copy-start | bytes 3962896
  25.1 32.0 %collective-permute-start = (f32[330241]{0:T(1024)}, f32[330241]{0:T(1024)S(1)}, u32[]{:S(2)}, u32[]{:S(2)}) collective-permute-start(f32[330241]{0:T(1024)} %concatenate.51), channel_id=1, source_target_pairs={{0,1},{1,2},{2,3},{3,4},{4,5},{5,6},{6,7},{7,8},{8,9},{9,10},{10,1... | collective-permute-start | bytes 3962900 | tf_op jit(solution)/shard_map/ppermute | solution.py:19
  58.2 30.8 %collective-permute-start.1 = (f32[330241]{0:T(1024)S(1)}, f32[330241]{0:T(1024)S(1)}, u32[]{:S(2)}, u32[]{:S(2)}) collective-permute-start(f32[330241]{0:T(1024)S(1)} %broadcast_select_fusion.1), channel_id=1, source_target_pairs={{0,1},{1,2},{2,3},{3,4},{4,5},{5,6},{6,7},{7,8},{8,9},{9,10},{10,1... | collective-permute-start | bytes 3962900 | tf_op jit(solution)/shard_map/ppermute | solution.py:19
  93.3 34.2 %copy-start.1 = (f32[330241]{0:T(1024)}, f32[330241]{0:T(1024)S(1)}, u32[]{:S(2)}) copy-start(f32[330241]{0:T(1024)S(1)} %maximum_select_fusion) | copy-start | bytes 3962896
  93.3 31.7 %collective-permute-start.2 = (f32[330241]{0:T(1024)S(1)}, f32[330241]{0:T(1024)}, u32[]{:S(2)}, u32[]{:S(2)}) collective-permute-start(f32[330241]{0:T(1024)S(1)} %maximum_select_fusion), channel_id=1, source_target_pairs={{0,2},{1,3},{2,4},{3,5},{4,6},{5,7},{6,8},{7,9},{8,10},{9,11},{10,... | collective-permute-start | bytes 3962900 | tf_op jit(solution)/shard_map/ppermute | solution.py:19
  132.1 33.4 %collective-permute-start.3 = (f32[330241]{0:T(1024)S(1)}, f32[330241]{0:T(1024)}, u32[]{:S(2)}, u32[]{:S(2)}) collective-permute-start(f32[330241]{0:T(1024)S(1)} %maximum_select_fusion.1), channel_id=1, source_target_pairs={{0,4},{1,5},{2,6},{3,7},{4,8},{5,9},{6,10},{7,11},{8,12},{9,13},{1... | collective-permute-start | bytes 3962900 | tf_op jit(solution)/shard_map/ppermute | solution.py:19
  172.3 48.9 %collective-permute-start.4 = (f32[330241]{0:T(1024)}, f32[330241]{0:T(1024)S(1)}, u32[]{:S(2)}, u32[]{:S(2)}) collective-permute-start(f32[330241]{0:T(1024)} %maximum_select_fusion.2), channel_id=1, source_target_pairs={{0,8},{1,9},{2,10},{3,11},{4,12},{5,13},{6,14},{7,15},{8,16},{9,17... | collective-permute-start | bytes 3962900 | tf_op jit(solution)/shard_map/ppermute | solution.py:19
  227.4 59.7 %collective-permute-start.5 = (f32[330241]{0:T(1024)S(1)}, f32[330241]{0:T(1024)}, u32[]{:S(2)}, u32[]{:S(2)}) collective-permute-start(f32[330241]{0:T(1024)S(1)} %maximum_select_fusion.3), channel_id=1, source_target_pairs={{0,16},{1,17},{2,18},{3,19},{4,20},{5,21},{6,22},{7,23},{8,24},{9,... | collective-permute-start | bytes 3962900 | tf_op jit(solution)/shard_map/ppermute | solution.py:19
  293.9 29.8 %collective-permute-start.6 = (f32[330241]{0:T(1024)}, f32[330241]{0:T(1024)S(1)}, u32[]{:S(2)}, u32[]{:S(2)}) collective-permute-start(f32[330241]{0:T(1024)} %maximum_select_fusion.4), channel_id=1, source_target_pairs={{0,32},{1,33},{2,34},{3,35},{4,36},{5,37},{6,38},{7,39},{8,40},{9,... | collective-permute-start | bytes 3962900 | tf_op jit(solution)/shard_map/ppermute | solution.py:19
  330.0 58.8 %collective-permute-start.7 = (f32[330241]{0:T(1024)S(1)}, f32[330241]{0:T(1024)}, u32[]{:S(2)}, u32[]{:S(2)}) collective-permute-start(f32[330241]{0:T(1024)S(1)} %maximum_select_fusion.5), channel_id=1, source_target_pairs={{0,64},{1,65},{2,66},{3,67},{4,68},{5,69},{6,70},{7,71},{8,72},{9,... | collective-permute-start | bytes 3962900 | tf_op jit(solution)/shard_map/ppermute | solution.py:19
  370.2 18.7 %copy-start.4 = (bf16[128,16,160]{0,2,1:T(8,128)(2,1)}, bf16[128,16,160]{0,2,1:T(8,128)(2,1)S(1)}, u32[]{:S(2)}) copy-start(bf16[128,16,160]{0,2,1:T(8,128)(2,1)S(1)} %get-tuple-element.38) | copy-start | bytes 1966084
  402.1 249.8 %copy-start.32 = (f32[128,16]{0,1:T(8,128)}, f32[128,16]{0,1:T(8,128)S(1)}, u32[]{:S(2)}) copy-start(f32[128,16]{0,1:T(8,128)S(1)} %fusion.67) | copy-start | bytes 24580
  423.0 30.5 %collective-permute-start.8 = (f32[330241]{0:T(1024)}, f32[330241]{0:T(1024)S(1)}, u32[]{:S(2)}, u32[]{:S(2)}) collective-permute-start(f32[330241]{0:T(1024)} %concatenate.59), channel_id=1, source_target_pairs={{1,0},{2,1},{3,2},{4,3},{5,4},{6,5},{7,6},{8,7},{9,8},{10,9},{11,1... | collective-permute-start | bytes 3962900 | tf_op jit(solution)/shard_map/ppermute | solution.py:19
  454.6 29.4 %collective-permute-start.9 = (f32[330241]{0:T(1024)S(1)}, f32[330241]{0:T(1024)S(1)}, u32[]{:S(2)}, u32[]{:S(2)}) collective-permute-start(f32[330241]{0:T(1024)S(1)} %broadcast_select_fusion), channel_id=1, source_target_pairs={{1,0},{2,1},{3,2},{4,3},{5,4},{6,5},{7,6},{8,7},{9,8},{10,9},{11,1... | collective-permute-start | bytes 3962900 | tf_op jit(solution)/shard_map/ppermute | solution.py:19
  488.2 30.1 %collective-permute-start.10 = (f32[330241]{0:T(1024)S(1)}, f32[330241]{0:T(1024)S(1)}, u32[]{:S(2)}, u32[]{:S(2)}) collective-permute-start(f32[330241]{0:T(1024)S(1)} %maximum_select_fusion.7), channel_id=1, source_target_pairs={{2,0},{3,1},{4,2},{5,3},{6,4},{7,5},{8,6},{9,7},{10,8},{11,9},{12,... | collective-permute-start | bytes 3962900 | tf_op jit(solution)/shard_map/ppermute | solution.py:19
  522.0 27.7 %collective-permute-start.11 = (f32[330241]{0:T(1024)S(1)}, f32[330241]{0:T(1024)S(1)}, u32[]{:S(2)}, u32[]{:S(2)}) collective-permute-start(f32[330241]{0:T(1024)S(1)} %maximum_select_fusion.8), channel_id=1, source_target_pairs={{4,0},{5,1},{6,2},{7,3},{8,4},{9,5},{10,6},{11,7},{12,8},{13,9},{1... | collective-permute-start | bytes 3962900 | tf_op jit(solution)/shard_map/ppermute | solution.py:19
  553.3 57.8 %collective-permute-start.12 = (f32[330241]{0:T(1024)S(1)}, f32[330241]{0:T(1024)S(1)}, u32[]{:S(2)}, u32[]{:S(2)}) collective-permute-start(f32[330241]{0:T(1024)S(1)} %maximum_select_fusion.9), channel_id=1, source_target_pairs={{8,0},{9,1},{10,2},{11,3},{12,4},{13,5},{14,6},{15,7},{16,8},{17,9... | collective-permute-start | bytes 3962900 | tf_op jit(solution)/shard_map/ppermute | solution.py:19
  614.8 32.1 %collective-permute-start.13 = (f32[330241]{0:T(1024)S(1)}, f32[330241]{0:T(1024)S(1)}, u32[]{:S(2)}, u32[]{:S(2)}) collective-permute-start(f32[330241]{0:T(1024)S(1)} %maximum_select_fusion.10), channel_id=1, source_target_pairs={{16,0},{17,1},{18,2},{19,3},{20,4},{21,5},{22,6},{23,7},{24,8},{25... | collective-permute-start | bytes 3962900 | tf_op jit(solution)/shard_map/ppermute | solution.py:19
  650.5 48.0 %collective-permute-start.14 = (f32[330241]{0:T(1024)S(1)}, f32[330241]{0:T(1024)S(1)}, u32[]{:S(2)}, u32[]{:S(2)}) collective-permute-start(f32[330241]{0:T(1024)S(1)} %maximum_select_fusion.11), channel_id=1, source_target_pairs={{32,0},{33,1},{34,2},{35,3},{36,4},{37,5},{38,6},{39,7},{40,8},{41... | collective-permute-start | bytes 3962900 | tf_op jit(solution)/shard_map/ppermute | solution.py:19
  702.3 50.3 %collective-permute-start.15 = (f32[330241]{0:T(1024)S(1)}, f32[330241]{0:T(1024)}, u32[]{:S(2)}, u32[]{:S(2)}) collective-permute-start(f32[330241]{0:T(1024)S(1)} %maximum_select_fusion.12), channel_id=1, source_target_pairs={{64,0},{65,1},{66,2},{67,3},{68,4},{69,5},{70,6},{71,7},{72,8},{73... | collective-permute-start | bytes 3962900 | tf_op jit(solution)/shard_map/ppermute | solution.py:19
  760.0 4.2 copy-start.18
  (28 other events, 65.7 us)
Sparse Core Ops, SparseCore 0:
  767.9 258.2 all-reduce.1
where the time goes:
time: 1050 us; the launch traced here: 1040 us
  waiting for transfers between devices  739 us (70%)
  starting transfers between devices  114 us (11%)
  local copies, waits for them, and re-layouts  66.3 us (6%)
  other arithmetic  49.1 us (5%)
  matrix products  35 us (3%)
  between operations  33.9 us (3%)
    ppermute x16, waiting for transfers between devices, passed_along(): return lax.ppermute(array, axis, pairs)  484 us
    psum x1, waiting for transfers between devices, shards(): weight_grad = lax.psum(weight_part, ('dp', 'ctx'))  255 us
    ppermute x16, starting transfers between devices, passed_along(): return lax.ppermute(array, axis, pairs)  114 us
    concatenate x2, local copies, waits for them, and re-layouts, pack_parts(): return jnp.concatenate([part.reshape(-1) for part in parts])  24.5 us
    select_n x14, other arithmetic, prefix(): total = jnp.where(valid(step), chain_combine(got, total), total)  21.1 us
  transfers between devices with their start and end apart: 17, of which 17 were waited for; matrix products, arithmetic and copies ran while one was open for 3% of the time, Pallas kernels for 0%

commit v1 on v0

--- a/solution.py
+++ b/solution.py
@@ -3,6 +3,7 @@
 import jax.numpy as jnp
 from jax import lax
 from jax.sharding import PartitionSpec as P
+from jax.lax import all_gather
 
 H = 16
 DH = 128
@@ -158,7 +159,7 @@
     weight_part = jnp.einsum(
         "thd,thf->df", query3, grad_pq, preferred_element_type=jnp.float32
     ) + jnp.einsum("thd,thf->df", key3, grad_pk, preferred_element_type=jnp.float32)
-    weight_grad = lax.psum(weight_part, ("dp", "ctx"))
+    weight_grad = jnp.sum(all_gather(weight_part, axis_name=("dp", "ctx")), 0)
     scale = lax.rsqrt(jnp.mean(weight_grad * weight_grad) + EPSILON)
     new_weight = feat_weight.astype(jnp.float32) - RATE * weight_grad * scale
     shape_out = (1, tokens, H * DH)

time: 1050 us -> 958 us (0.912)
  waiting for transfers between devices: 739 us -> 632 us
  local copies, waits for them, and re-layouts: 66.3 us -> 79 us
  starting transfers between devices: 114 us -> 125 us
    psum x1 -> x0, waiting for transfers between devices: 255 us -> none  [shards(): weight_grad = lax.psum(weight_part, ('dp', 'ctx'))]
    all_gather x0 -> x1, waiting for transfers between devices: none -> 149 us  [shards(): weight_grad = jnp.sum(all_gather(weight_part, axis_name=('dp', 'ctx')), 0)]
    unnamed x77 -> x62, local copies, waits for them, and re-layouts: 14.8 us -> 28.2 us
    ppermute x16, starting transfers between devices: 114 us -> 124 us  [passed_along(): return lax.ppermute(array, axis, pairs)]
  transfers between devices with their start and end apart: 17 -> 17, of which waited for: 17 -> 17; matrix products, arithmetic and copies ran while one was open for 3% -> 4% of each run, Pallas kernels for 0% -> 0%
where the time goes in v1:
time: 958 us; the launch traced here: 948 us
  waiting for transfers between devices  632 us (66%)
  starting transfers between devices  125 us (13%)
  local copies, waits for them, and re-layouts  79 us (8%)
  other arithmetic  48.2 us (5%)
  between operations  33.3 us (3%)
  matrix products  30.9 us (3%)
    ppermute x16, waiting for transfers between devices, passed_along(): return lax.ppermute(array, axis, pairs)  483 us
    all_gather x1, waiting for transfers between devices, shards(): weight_grad = jnp.sum(all_gather(weight_part, axis_name=('dp', 'ctx')), 0)  149 us
    ppermute x16, starting transfers between devices, passed_along(): return lax.ppermute(array, axis, pairs)  124 us
    unnamed x62, local copies, waits for them, and re-layouts  28.2 us
    concatenate x2, local copies, waits for them, and re-layouts, pack_parts(): return jnp.concatenate([part.reshape(-1) for part in parts])  24.5 us
    select_n x14, other arithmetic, prefix(): total = jnp.where(valid(step), chain_combine(got, total), total)  20.9 us
  transfers between devices with their start and end apart: 17, of which 17 were waited for; matrix products, arithmetic and copies ran while one was open for 4% of the time, Pallas kernels for 0%

profile of v1, /device:TPU:1, one launch (start us, length us, event | category | flops | bytes accessed | tf_op | source)
XLA Modules:
  0.0 947.8 jit_solution(16744019342575722094)
XLA Ops:
  14.4 10.6 %concatenate.51 = f32[330241]{0:T(1024)} concatenate(f32[1]{0:T(128)} %get-tuple-element.35, f32[327680]{0:T(1024)S(1)} %bitcast.142, f32[2560]{0:T(1024)S(1)} %convolution_reduce_fusion), dimensions={0} | concatenate | bytes 2641928 | tf_op jit(solution)/shard_map/concatenate | solution.py:28
  29.1 27.9 %collective-permute-done = f32[330241]{0:T(1024)S(1)} collective-permute-done((f32[330241]{0:T(1024)}, f32[330241]{0:T(1024)S(1)}, u32[]{:S(2)}, u32[]{:S(2)}) %collective-permute-start) | collective-permute-done | bytes 1320996 | tf_op jit(solution)/shard_map/ppermute | solution.py:20
  62.7 26.3 %collective-permute-done.1 = f32[330241]{0:T(1024)S(1)} collective-permute-done((f32[330241]{0:T(1024)S(1)}, f32[330241]{0:T(1024)S(1)}, u32[]{:S(2)}, u32[]{:S(2)}) %collective-permute-start.1) | collective-permute-done | bytes 1320996 | tf_op jit(solution)/shard_map/ppermute | solution.py:20
  93.2 6.8 collective-permute-start.2
  100.5 24.4 %collective-permute-done.2 = f32[330241]{0:T(1024)} collective-permute-done((f32[330241]{0:T(1024)S(1)}, f32[330241]{0:T(1024)}, u32[]{:S(2)}, u32[]{:S(2)}) %collective-permute-start.2) | collective-permute-done | bytes 1320996 | tf_op jit(solution)/shard_map/ppermute | solution.py:20
  132.0 9.3 collective-permute-start.3
  141.8 23.5 %collective-permute-done.3 = f32[330241]{0:T(1024)} collective-permute-done((f32[330241]{0:T(1024)S(1)}, f32[330241]{0:T(1024)}, u32[]{:S(2)}, u32[]{:S(2)}) %collective-permute-start.3) | collective-permute-done | bytes 1320996 | tf_op jit(solution)/shard_map/ppermute | solution.py:20
  179.0 42.0 %collective-permute-done.4 = f32[330241]{0:T(1024)S(1)} collective-permute-done((f32[330241]{0:T(1024)}, f32[330241]{0:T(1024)S(1)}, u32[]{:S(2)}, u32[]{:S(2)}) %collective-permute-start.4) | collective-permute-done | bytes 1320996 | tf_op jit(solution)/shard_map/ppermute | solution.py:20
  227.3 25.8 %collective-permute-start.5 = (f32[330241]{0:T(1024)S(1)}, f32[330241]{0:T(1024)}, u32[]{:S(2)}, u32[]{:S(2)}) collective-permute-start(f32[330241]{0:T(1024)S(1)} %maximum_select_fusion.3), channel_id=1, source_target_pairs={{0,16},{1,17},{2,18},{3,19},{4,20},{5,21},{6,22},{7,23},{8,24},{9,... | collective-permute-start | bytes 3962900 | tf_op jit(solution)/shard_map/ppermute | solution.py:20
  253.6 33.4 %collective-permute-done.5 = f32[330241]{0:T(1024)} collective-permute-done((f32[330241]{0:T(1024)S(1)}, f32[330241]{0:T(1024)}, u32[]{:S(2)}, u32[]{:S(2)}) %collective-permute-start.5) | collective-permute-done | bytes 1320996 | tf_op jit(solution)/shard_map/ppermute | solution.py:20
  293.7 13.6 %collective-permute-start.6 = (f32[330241]{0:T(1024)}, f32[330241]{0:T(1024)S(1)}, u32[]{:S(2)}, u32[]{:S(2)}) collective-permute-start(f32[330241]{0:T(1024)} %maximum_select_fusion.4), channel_id=1, source_target_pairs={{0,32},{1,33},{2,34},{3,35},{4,36},{5,37},{6,38},{7,39},{8,40},{9,... | collective-permute-start | bytes 3962900 | tf_op jit(solution)/shard_map/ppermute | solution.py:20
  308.6 15.0 %collective-permute-done.6 = f32[330241]{0:T(1024)S(1)} collective-permute-done((f32[330241]{0:T(1024)}, f32[330241]{0:T(1024)S(1)}, u32[]{:S(2)}, u32[]{:S(2)}) %collective-permute-start.6) | collective-permute-done | bytes 1320996 | tf_op jit(solution)/shard_map/ppermute | solution.py:20
  329.8 44.6 %collective-permute-start.7 = (f32[330241]{0:T(1024)S(1)}, f32[330241]{0:T(1024)}, u32[]{:S(2)}, u32[]{:S(2)}) collective-permute-start(f32[330241]{0:T(1024)S(1)} %maximum_select_fusion.5), channel_id=1, source_target_pairs={{0,64},{1,65},{2,66},{3,67},{4,68},{5,69},{6,70},{7,71},{8,72},{9,... | collective-permute-start | bytes 3962900 | tf_op jit(solution)/shard_map/ppermute | solution.py:20
  408.6 13.9 %concatenate.59 = f32[330241]{0:T(1024)} concatenate(f32[1]{0:T(128)} %get-tuple-element.34, f32[327680]{0:T(1024)} %bitcast.155, f32[2560]{0:T(1024)S(1)} %reshape.197), dimensions={0} | concatenate | bytes 2641928 | tf_op jit(solution)/shard_map/concatenate | solution.py:28
  423.8 29.2 %collective-permute-done.8 = f32[330241]{0:T(1024)S(1)} collective-permute-done((f32[330241]{0:T(1024)}, f32[330241]{0:T(1024)S(1)}, u32[]{:S(2)}, u32[]{:S(2)}) %collective-permute-start.8) | collective-permute-done | bytes 1320996 | tf_op jit(solution)/shard_map/ppermute | solution.py:20
  455.9 27.6 %collective-permute-done.9 = f32[330241]{0:T(1024)S(1)} collective-permute-done((f32[330241]{0:T(1024)S(1)}, f32[330241]{0:T(1024)S(1)}, u32[]{:S(2)}, u32[]{:S(2)}) %collective-permute-start.9) | collective-permute-done | bytes 1320996 | tf_op jit(solution)/shard_map/ppermute | solution.py:20
  489.4 28.3 %collective-permute-done.10 = f32[330241]{0:T(1024)S(1)} collective-permute-done((f32[330241]{0:T(1024)S(1)}, f32[330241]{0:T(1024)S(1)}, u32[]{:S(2)}, u32[]{:S(2)}) %collective-permute-start.10) | collective-permute-done | bytes 1320996 | tf_op jit(solution)/shard_map/ppermute | solution.py:20
  523.1 25.9 %collective-permute-done.11 = f32[330241]{0:T(1024)S(1)} collective-permute-done((f32[330241]{0:T(1024)S(1)}, f32[330241]{0:T(1024)S(1)}, u32[]{:S(2)}, u32[]{:S(2)}) %collective-permute-start.11) | collective-permute-done | bytes 1320996 | tf_op jit(solution)/shard_map/ppermute | solution.py:20
  554.3 55.9 %collective-permute-done.12 = f32[330241]{0:T(1024)S(1)} collective-permute-done((f32[330241]{0:T(1024)S(1)}, f32[330241]{0:T(1024)S(1)}, u32[]{:S(2)}, u32[]{:S(2)}) %collective-permute-start.12) | collective-permute-done | bytes 1320996 | tf_op jit(solution)/shard_map/ppermute | solution.py:20
  615.7 30.3 %collective-permute-done.13 = f32[330241]{0:T(1024)S(1)} collective-permute-done((f32[330241]{0:T(1024)S(1)}, f32[330241]{0:T(1024)S(1)}, u32[]{:S(2)}, u32[]{:S(2)}) %collective-permute-start.13) | collective-permute-done | bytes 1320996 | tf_op jit(solution)/shard_map/ppermute | solution.py:20
  651.4 46.1 %collective-permute-done.14 = f32[330241]{0:T(1024)S(1)} collective-permute-done((f32[330241]{0:T(1024)S(1)}, f32[330241]{0:T(1024)S(1)}, u32[]{:S(2)}, u32[]{:S(2)}) %collective-permute-start.14) | collective-permute-done | bytes 1320996 | tf_op jit(solution)/shard_map/ppermute | solution.py:20
  709.7 41.4 %collective-permute-done.15 = f32[330241]{0:T(1024)S(1)} collective-permute-done((f32[330241]{0:T(1024)S(1)}, f32[330241]{0:T(1024)S(1)}, u32[]{:S(2)}, u32[]{:S(2)}) %collective-permute-start.15) | collective-permute-done | bytes 1320996 | tf_op jit(solution)/shard_map/ppermute | solution.py:20
  775.6 149.1 %all-gather.3.cloned.1.call-done = f32[32768,160]{0,1:T(8,128)} async-done(((f32[128,160]{0,1:T(8,128)}), f32[32768,160]{0,1:T(8,128)}) %all-gather.3.cloned.1.call-update) | async-done | bytes 20971536 | tf_op jit(solution)/shard_map/all_gather | solution.py:162
  924.6 11.5 %copy.47 = f32[20,8,256,128]{3,2,1,0:T(8,128)S(1)} copy(f32[20,8,256,128]{3,1,2,0:T(8,128)} %bitcast.137) | data formatting | bytes 41943040
  (185 shorter events, 152.0 us)
Async XLA Ops:
  7.2 5.4 copy-start.25
  7.2 5.5 copy-start.24
  7.2 917.5 %all-gather.3.cloned.1.call-start = ((), (), s32[]{:S(2)}) async-start(), calls=%async_computation | async-start | bytes 21053440 | tf_op jit(solution)/shard_map/all_gather | solution.py:162
  14.4 42.7 %copy-start = (f32[330241]{0:T(1024)S(1)}, f32[330241]{0:T(1024)}, u32[]{:S(2)}) copy-start(f32[330241]{0:T(1024)} %constant.75.clone.1) | copy-start | bytes 3962896
  25.0 32.0 %collective-permute-start = (f32[330241]{0:T(1024)}, f32[330241]{0:T(1024)S(1)}, u32[]{:S(2)}, u32[]{:S(2)}) collective-permute-start(f32[330241]{0:T(1024)} %concatenate.51), channel_id=1, source_target_pairs={{0,1},{1,2},{2,3},{3,4},{4,5},{5,6},{6,7},{7,8},{8,9},{9,10},{10,1... | collective-permute-start | bytes 3962900 | tf_op jit(solution)/shard_map/ppermute | solution.py:20
  58.1 30.8 %collective-permute-start.1 = (f32[330241]{0:T(1024)S(1)}, f32[330241]{0:T(1024)S(1)}, u32[]{:S(2)}, u32[]{:S(2)}) collective-permute-start(f32[330241]{0:T(1024)S(1)} %broadcast_select_fusion.1), channel_id=1, source_target_pairs={{0,1},{1,2},{2,3},{3,4},{4,5},{5,6},{6,7},{7,8},{8,9},{9,10},{10,1... | collective-permute-start | bytes 3962900 | tf_op jit(solution)/shard_map/ppermute | solution.py:20
  93.2 34.2 %copy-start.1 = (f32[330241]{0:T(1024)}, f32[330241]{0:T(1024)S(1)}, u32[]{:S(2)}) copy-start(f32[330241]{0:T(1024)S(1)} %maximum_select_fusion) | copy-start | bytes 3962896
  93.2 31.7 %collective-permute-start.2 = (f32[330241]{0:T(1024)S(1)}, f32[330241]{0:T(1024)}, u32[]{:S(2)}, u32[]{:S(2)}) collective-permute-start(f32[330241]{0:T(1024)S(1)} %maximum_select_fusion), channel_id=1, source_target_pairs={{0,2},{1,3},{2,4},{3,5},{4,6},{5,7},{6,8},{7,9},{8,10},{9,11},{10,... | collective-permute-start | bytes 3962900 | tf_op jit(solution)/shard_map/ppermute | solution.py:20
  132.0 33.4 %collective-permute-start.3 = (f32[330241]{0:T(1024)S(1)}, f32[330241]{0:T(1024)}, u32[]{:S(2)}, u32[]{:S(2)}) collective-permute-start(f32[330241]{0:T(1024)S(1)} %maximum_select_fusion.1), channel_id=1, source_target_pairs={{0,4},{1,5},{2,6},{3,7},{4,8},{5,9},{6,10},{7,11},{8,12},{9,13},{1... | collective-permute-start | bytes 3962900 | tf_op jit(solution)/shard_map/ppermute | solution.py:20
  172.1 48.9 %collective-permute-start.4 = (f32[330241]{0:T(1024)}, f32[330241]{0:T(1024)S(1)}, u32[]{:S(2)}, u32[]{:S(2)}) collective-permute-start(f32[330241]{0:T(1024)} %maximum_select_fusion.2), channel_id=1, source_target_pairs={{0,8},{1,9},{2,10},{3,11},{4,12},{5,13},{6,14},{7,15},{8,16},{9,17... | collective-permute-start | bytes 3962900 | tf_op jit(solution)/shard_map/ppermute | solution.py:20
  227.3 59.7 %collective-permute-start.5 = (f32[330241]{0:T(1024)S(1)}, f32[330241]{0:T(1024)}, u32[]{:S(2)}, u32[]{:S(2)}) collective-permute-start(f32[330241]{0:T(1024)S(1)} %maximum_select_fusion.3), channel_id=1, source_target_pairs={{0,16},{1,17},{2,18},{3,19},{4,20},{5,21},{6,22},{7,23},{8,24},{9,... | collective-permute-start | bytes 3962900 | tf_op jit(solution)/shard_map/ppermute | solution.py:20
  293.7 29.8 %collective-permute-start.6 = (f32[330241]{0:T(1024)}, f32[330241]{0:T(1024)S(1)}, u32[]{:S(2)}, u32[]{:S(2)}) collective-permute-start(f32[330241]{0:T(1024)} %maximum_select_fusion.4), channel_id=1, source_target_pairs={{0,32},{1,33},{2,34},{3,35},{4,36},{5,37},{6,38},{7,39},{8,40},{9,... | collective-permute-start | bytes 3962900 | tf_op jit(solution)/shard_map/ppermute | solution.py:20
  329.8 58.8 %collective-permute-start.7 = (f32[330241]{0:T(1024)S(1)}, f32[330241]{0:T(1024)}, u32[]{:S(2)}, u32[]{:S(2)}) collective-permute-start(f32[330241]{0:T(1024)S(1)} %maximum_select_fusion.5), channel_id=1, source_target_pairs={{0,64},{1,65},{2,66},{3,67},{4,68},{5,69},{6,70},{7,71},{8,72},{9,... | collective-permute-start | bytes 3962900 | tf_op jit(solution)/shard_map/ppermute | solution.py:20
  381.2 7.5 copy-start.4
  398.2 3.4 copy-start.20
  422.5 30.5 %collective-permute-start.8 = (f32[330241]{0:T(1024)}, f32[330241]{0:T(1024)S(1)}, u32[]{:S(2)}, u32[]{:S(2)}) collective-permute-start(f32[330241]{0:T(1024)} %concatenate.59), channel_id=1, source_target_pairs={{1,0},{2,1},{3,2},{4,3},{5,4},{6,5},{7,6},{8,7},{9,8},{10,9},{11,1... | collective-permute-start | bytes 3962900 | tf_op jit(solution)/shard_map/ppermute | solution.py:20
  454.1 29.4 %collective-permute-start.9 = (f32[330241]{0:T(1024)S(1)}, f32[330241]{0:T(1024)S(1)}, u32[]{:S(2)}, u32[]{:S(2)}) collective-permute-start(f32[330241]{0:T(1024)S(1)} %broadcast_select_fusion), channel_id=1, source_target_pairs={{1,0},{2,1},{3,2},{4,3},{5,4},{6,5},{7,6},{8,7},{9,8},{10,9},{11,1... | collective-permute-start | bytes 3962900 | tf_op jit(solution)/shard_map/ppermute | solution.py:20
  487.6 30.1 %collective-permute-start.10 = (f32[330241]{0:T(1024)S(1)}, f32[330241]{0:T(1024)S(1)}, u32[]{:S(2)}, u32[]{:S(2)}) collective-permute-start(f32[330241]{0:T(1024)S(1)} %maximum_select_fusion.7), channel_id=1, source_target_pairs={{2,0},{3,1},{4,2},{5,3},{6,4},{7,5},{8,6},{9,7},{10,8},{11,9},{12,... | collective-permute-start | bytes 3962900 | tf_op jit(solution)/shard_map/ppermute | solution.py:20
  521.3 27.7 %collective-permute-start.11 = (f32[330241]{0:T(1024)S(1)}, f32[330241]{0:T(1024)S(1)}, u32[]{:S(2)}, u32[]{:S(2)}) collective-permute-start(f32[330241]{0:T(1024)S(1)} %maximum_select_fusion.8), channel_id=1, source_target_pairs={{4,0},{5,1},{6,2},{7,3},{8,4},{9,5},{10,6},{11,7},{12,8},{13,9},{1... | collective-permute-start | bytes 3962900 | tf_op jit(solution)/shard_map/ppermute | solution.py:20
  552.5 57.7 %collective-permute-start.12 = (f32[330241]{0:T(1024)S(1)}, f32[330241]{0:T(1024)S(1)}, u32[]{:S(2)}, u32[]{:S(2)}) collective-permute-start(f32[330241]{0:T(1024)S(1)} %maximum_select_fusion.9), channel_id=1, source_target_pairs={{8,0},{9,1},{10,2},{11,3},{12,4},{13,5},{14,6},{15,7},{16,8},{17,9... | collective-permute-start | bytes 3962900 | tf_op jit(solution)/shard_map/ppermute | solution.py:20
  613.9 32.1 %collective-permute-start.13 = (f32[330241]{0:T(1024)S(1)}, f32[330241]{0:T(1024)S(1)}, u32[]{:S(2)}, u32[]{:S(2)}) collective-permute-start(f32[330241]{0:T(1024)S(1)} %maximum_select_fusion.10), channel_id=1, source_target_pairs={{16,0},{17,1},{18,2},{19,3},{20,4},{21,5},{22,6},{23,7},{24,8},{25... | collective-permute-start | bytes 3962900 | tf_op jit(solution)/shard_map/ppermute | solution.py:20
  649.5 47.9 %collective-permute-start.14 = (f32[330241]{0:T(1024)S(1)}, f32[330241]{0:T(1024)S(1)}, u32[]{:S(2)}, u32[]{:S(2)}) collective-permute-start(f32[330241]{0:T(1024)S(1)} %maximum_select_fusion.11), channel_id=1, source_target_pairs={{32,0},{33,1},{34,2},{35,3},{36,4},{37,5},{38,6},{39,7},{40,8},{41... | collective-permute-start | bytes 3962900 | tf_op jit(solution)/shard_map/ppermute | solution.py:20
  701.0 50.1 %collective-permute-start.15 = (f32[330241]{0:T(1024)S(1)}, f32[330241]{0:T(1024)S(1)}, u32[]{:S(2)}, u32[]{:S(2)}) collective-permute-start(f32[330241]{0:T(1024)S(1)} %maximum_select_fusion.12), channel_id=1, source_target_pairs={{64,0},{65,1},{66,2},{67,3},{68,4},{69,5},{70,6},{71,7},{72,8},{73... | collective-permute-start | bytes 3962900 | tf_op jit(solution)/shard_map/ppermute | solution.py:20
  756.7 3.7 copy-start.17
  (20 other events, 31.7 us)
Sparse Core Ops, SparseCore 0:
  762.8 161.7 all-gather.2
